TPU v7x, 32 devices: a whole 2x2x4 slice. The times are simulated.
32 devices in a mesh: grp: 4 (over y, x), wide: 8 (over z, core).
Axes of the slice: x: 2, y: 2, z: 4, core: 2. Of those that a mesh axis runs over, the one named last changes fastest.
Arguments:
- spectral: float32 [8, 48, 320, 2, 641], P(None, 'grp', 'wide'), may hold values from -0.006 to 0.006
- legendre: float32 [320, 641, 320], P('wide'), may hold values from -18 to 18
- pair_table: int32 [320], replicated, may hold values from 0 to 319, each once
- field_map: int32 [8], replicated, may hold values from 0 to 7, each once
Outputs:
- grid_values: float32 [8, 48, 640, 1280], P('grp', None, 'wide')
- checksums: float32 [8, 48], replicated
Inputs may be any that keep to these rules, and one draw needn't show every extreme that they name: Each slot number appears once; slot s holds wavenumbers pair_table[s] and 639 - pair_table[s]. `field_map`: each field appears once.
All inputs are finite; a program needn't handle non-finite values.
Results may differ from a plain program's by a relative error of at most 0.000078.
Values sent between devices are 32-bit elements; how exact they have to be, the bound alone decides.
No kernel may reach another device: no remote copies, remote signals or barrier semaphores. Data moves between devices by JAX's collectives and lax.ppermute only.
A program may use at most 448 MiB of HBM per device.

v0:
```python
import math

import jax
import jax.numpy as jnp
from jax import lax
from jax.sharding import PartitionSpec as P

WAVES = 640
LAT = 640
LON = 1280


HIGHEST = lax.Precision.HIGHEST


def passed_along(value, axis, steps):
    count = lax.axis_size(axis)
    pairs = [(source, (source + steps) % count) for source in range(count)]
    return lax.ppermute(value, axis, pairs)


def legendre_table(legendre, slot_pairs):
    slot_count = legendre.shape[0]
    coeff_count = legendre.shape[1]
    degree = jnp.arange(coeff_count, dtype=jnp.int32)[None, :]
    boundary = (WAVES - slot_pairs)[:, None]
    first_part = degree < boundary
    belong = jnp.stack([first_part, ~first_part], 2).astype(jnp.float32)
    sign_first = jnp.broadcast_to(jnp.where(degree % 2 == 0, 1.0, -1.0), (slot_count, coeff_count))
    sign_second = jnp.where((degree - boundary) % 2 == 0, 1.0, -1.0)
    signs = jnp.stack([sign_first, sign_second], 2).astype(jnp.float32)
    north = belong[..., None] * legendre[:, :, None, :]
    south = (belong * signs)[..., None] * jnp.flip(legendre, -1)[:, :, None, :]
    return jnp.concatenate([north, south], -1)


def legendre_sums(coeffs, table):
    return lax.dot_general(
        coeffs,
        table,
        (((4,), (1,)), ((2,), (0,))),
        precision=HIGHEST,
        preferred_element_type=jnp.float32,
    )


def synthesis_table(pair_table):
    numbers = jnp.stack([pair_table, WAVES - 1 - pair_table], 1)
    columns = jnp.arange(LON, dtype=jnp.int32)
    phases = numbers[:, :, None] * columns % LON
    angles = phases.astype(jnp.float32) * (2.0 * math.pi / LON)
    factor = jnp.where(numbers == 0, 1.0, 2.0).astype(jnp.float32)[:, :, None]
    return jnp.stack([factor * jnp.cos(angles), -factor * jnp.sin(angles)], 1)


def local(spectral, legendre, pair_table, field_map):
    slot_count = legendre.shape[0]
    groups = lax.axis_size("grp")
    own_pairs = lax.dynamic_slice_in_dim(
        pair_table, lax.axis_index("wide") * slot_count, slot_count
    )
    ordered = jnp.take(spectral, field_map, axis=0)
    table = legendre_table(legendre, own_pairs)
    per_group = ordered.shape[0] // groups
    levels_here = ordered.shape[1]
    own_group = lax.axis_index("grp")
    arrived = None
    for offset in range(groups):
        target = (own_group + offset) % groups
        fields_part = lax.dynamic_slice_in_dim(ordered, target * per_group, per_group, 0)
        fourier = legendre_sums(fields_part, table)
        banded = lax.all_to_all(fourier, "wide", split_axis=5, concat_axis=0, tiled=True)
        if offset > 0:
            banded = passed_along(banded, "grp", offset)
        if arrived is None:
            shape_now = banded.shape
            arrived = jnp.zeros(
                (
                    shape_now[0],
                    shape_now[1],
                    shape_now[2] * groups,
                    shape_now[3],
                    shape_now[4],
                    shape_now[5],
                ),
                jnp.float32,
            )
        source = (own_group - offset) % groups
        arrived = lax.dynamic_update_slice_in_dim(arrived, banded, source * levels_here, 2)
    synthesis = synthesis_table(pair_table)
    gridded = lax.dot_general(
        arrived,
        synthesis,
        (((0, 3, 4), (0, 1, 2)), ((), ())),
        precision=HIGHEST,
        preferred_element_type=jnp.float32,
    )
    local_sum = jnp.sum(gridded * gridded, axis=(2, 3))
    summed = lax.psum(local_sum, "wide")
    checksums = lax.all_gather(summed, "grp", axis=0, tiled=True) / (LAT * LON)
    return (gridded, checksums)


def solution(mesh):
    placed = (P(None, "grp", "wide", None, None), P("wide", None, None), P(), P())
    return jax.shard_map(
        local,
        mesh=mesh,
        in_specs=placed,
        out_specs=(P("grp", None, "wide", None), P()),
        check_vma=False,
    )
```

profile of v0, /device:TPU:0, one launch (start us, length us, event | category | flops | bytes accessed | tf_op | source)
XLA Modules:
  0.0 2617.8 jit_solution(9344468815469829939)
XLA Ops:
  2.2 347.7 %rev.4 = f32[40,641,320]{1,2,0:T(8,128)} reverse(f32[40,641,320]{1,2,0:T(8,128)} %param.5), dimensions={2} | reverse | bytes 65638400 | tf_op jit(solution)/shard_map/jit(_flip)/rev | solution.py:33
  350.0 40.4 %copy.47 = f32[40,641,320]{2,1,0:T(8,128)} copy(f32[40,641,320]{1,2,0:T(8,128)} %param.5) | data formatting | bytes 65638400 | tf_op args[1]
  390.4 40.5 %copy.48 = f32[40,641,320]{2,1,0:T(8,128)} copy(f32[40,641,320]{1,2,0:T(8,128)} %rev.4) | data formatting | bytes 65638400 | tf_op jit(solution)/shard_map/jit(_flip)/rev | solution.py:33
  431.8 45.8 %gather_fusion = f32[8,12,40,2,641]{4,3,2,1,0:T(2,128)} fusion(f32[8,12,40,2,641]{4,3,2,1,0:T(2,128)} %param.4, s32[1024]{0:T(1024)S(1)} %pad_clamp_fusion), kind=kCustom, calls=%fused_computation | custom fusion | bytes 39383072 | tf_op jit(solution)/shard_map/jit(_take)/gather | solution.py:62
  477.6 26.9 %copy_select_fusion = f32[8,12,40,2,641]{4,1,3,0,2:T(8,128)} fusion(f32[8,12,40,2,641]{4,3,2,1,0:T(2,128)} %gather_fusion, pred[8]{0:T(512)(128)(4,1)S(1)} %compare_and_fusion), kind=kLoop, calls=%fused_computation.6 | loop fusion | flops 4922880 | bytes 39383048 | tf_op jit(solution)/shard_map/jit(_take)/select_n | solution.py:62
  504.4 79.1 %broadcast_multiply_fusion = (f32[40,641,2,320]{3,1,2,0:T(8,128)}, f32[40,641,2,320]{3,1,2,0:T(8,128)}) fusion(f32[40,641,320]{2,1,0:T(8,128)} %copy.48, f32[40,641,2]{1,2,0:T(2,128)S(1)} %maximum_select_fusion, f32[40,641,320]{2,1,0:T(8,128)} %copy.47, f32[40,641,2]{1,2,0:T(2,128)S(1)} %fusion.36), kind=kLoop, calls=%fused_computation.2 | loop fusion | flops 32819200 | bytes 197325440 | tf_op jit(solution)/shard_map/mul | solution.py:33
  583.5 95.5 %fusion.2 = f32[40,2,12,2,2,640]{5,2,4,3,1,0:T(8,128)} fusion(f32[40,641,2,320]{3,1,2,0:T(8,128)} %get-tuple-element.10, f32[40,641,2,320]{3,1,2,0:T(8,128)} %get-tuple-element.11, f32[8,12,40,2,641]{4,1,3,0,2:T(8,128)} %copy_select_fusion, s32[]{:T(128)S(6)} %select_n.154), kind=kOutput, calls=%fused_computation.9 | convolution fusion | flops 18936678400 | bytes 176947200 | tf_op jit(solution)/shard_map/dot_general | solution.py:38
  679.0 36.1 %copy.53 = f32[40,2,12,2,2,640]{0,4,3,2,1,5:T(2,128)} copy(f32[40,2,12,2,2,640]{5,2,4,3,1,0:T(8,128)} %fusion.2) | data formatting | bytes 19660800 | tf_op jit(solution)/shard_map/dot_general | solution.py:38
  715.1 62.9 %reshape.304 = f32[8,1,307200]{2,1,0:T(1,128)} reshape(f32[640,2,12,2,2,40]{5,4,3,2,1,0:T(2,128)} %bitcast.81) | data formatting | bytes 19660800
  784.8 95.2 %fusion.1 = f32[40,2,12,2,2,640]{5,2,4,3,1,0:T(8,128)} fusion(f32[40,641,2,320]{3,1,2,0:T(8,128)} %get-tuple-element.10, f32[40,641,2,320]{3,1,2,0:T(8,128)} %get-tuple-element.11, f32[8,12,40,2,641]{4,1,3,0,2:T(8,128)} %copy_select_fusion, s32[]{:T(128)S(6)} %select_n.158), kind=kOutput, calls=%fused_computation.8 | convolution fusion | flops 18936678400 | bytes 176947200 | tf_op jit(solution)/shard_map/dot_general | solution.py:38
  880.1 36.1 %copy.57 = f32[40,2,12,2,2,640]{0,4,3,2,1,5:T(2,128)} copy(f32[40,2,12,2,2,640]{5,2,4,3,1,0:T(8,128)} %fusion.1) | data formatting | bytes 19660800 | tf_op jit(solution)/shard_map/dot_general | solution.py:38
  916.2 62.9 %reshape.306 = f32[8,1,307200]{2,1,0:T(1,128)} reshape(f32[640,2,12,2,2,40]{5,4,3,2,1,0:T(2,128)} %bitcast.82) | data formatting | bytes 19660800
  1005.0 95.3 %fusion = f32[40,2,12,2,2,640]{5,2,4,3,1,0:T(8,128)} fusion(f32[40,641,2,320]{3,1,2,0:T(8,128)} %get-tuple-element.10, f32[40,641,2,320]{3,1,2,0:T(8,128)} %get-tuple-element.11, f32[8,12,40,2,641]{4,1,3,0,2:T(8,128)} %copy_select_fusion, s32[]{:T(128)S(6)} %select_n.162), kind=kOutput, calls=%fused_computation.7 | convolution fusion | flops 18936678400 | bytes 176947200 | tf_op jit(solution)/shard_map/dot_general | solution.py:38
  1100.3 36.1 %copy.61 = f32[40,2,12,2,2,640]{0,4,3,2,1,5:T(2,128)} copy(f32[40,2,12,2,2,640]{5,2,4,3,1,0:T(8,128)} %fusion) | data formatting | bytes 19660800 | tf_op jit(solution)/shard_map/dot_general | solution.py:38
  1136.4 62.9 %reshape.308 = f32[8,1,307200]{2,1,0:T(1,128)} reshape(f32[640,2,12,2,2,40]{5,4,3,2,1,0:T(2,128)} %bitcast.83) | data formatting | bytes 19660800
  1225.3 95.2 %fusion.3 = f32[40,2,12,2,2,640]{5,2,4,3,1,0:T(8,128)} fusion(f32[40,641,2,320]{3,1,2,0:T(8,128)} %get-tuple-element.10, f32[40,641,2,320]{3,1,2,0:T(8,128)} %get-tuple-element.11, f32[8,12,40,2,641]{4,1,3,0,2:T(8,128)} %copy_select_fusion, s32[]{:T(128)S(6)} %select_n.146), kind=kOutput, calls=%fused_computation.10 | convolution fusion | flops 18936678400 | bytes 176947200 | tf_op jit(solution)/shard_map/dot_general | solution.py:38
  1320.5 35.5 %copy.49 = f32[40,2,12,2,2,640]{0,4,3,2,1,5:T(2,128)} copy(f32[40,2,12,2,2,640]{5,2,4,3,1,0:T(8,128)} %fusion.3) | data formatting | bytes 19660800 | tf_op jit(solution)/shard_map/dot_general | solution.py:38
  1356.0 62.9 %reshape.302 = f32[8,1,307200]{2,1,0:T(1,128)} reshape(f32[640,2,12,2,2,40]{5,4,3,2,1,0:T(2,128)} %bitcast.84) | data formatting | bytes 19660800
  1418.9 21.1 all-to-all-done.3
  1445.8 90.6 %reduce.1 = f32[8,307200]{1,0:T(8,128)} reduce(f32[8,1,307200]{2,1,0:T(1,128)} %all-to-all-done.1, f32[]{:T(128)} %broadcast.351), dimensions={1}, to_apply=%all_to_all.56.reduce_sub_computation | reduce | bytes 19660804 | tf_op jit(solution)/shard_map/all_to_all | solution.py:72
  1536.4 83.9 %reshape.305 = f32[640,2,12,2,2,40]{5,4,3,2,1,0:T(2,128)} reshape(f32[8,307200]{1,0:T(8,128)} %reduce.1) | data formatting | bytes 19660800
  1620.3 36.9 %copy.75 = f32[40,2,12,2,2,8,80]{6,0,5,4,3,2,1:T(8,128)} copy(f32[40,2,12,2,2,8,80]{0,4,3,2,1,6,5:T(2,128)} %bitcast.85) | data formatting | bytes 19660800 | tf_op jit(solution)/shard_map/all_to_all | solution.py:72
  1674.4 90.9 %reduce.2 = f32[8,307200]{1,0:T(8,128)} reduce(f32[8,1,307200]{2,1,0:T(1,128)} %all-to-all-done.2, f32[]{:T(128)} %broadcast.351), dimensions={1}, to_apply=%all_to_all.60.reduce_sub_computation | reduce | bytes 19660804 | tf_op jit(solution)/shard_map/all_to_all | solution.py:72
  1765.3 83.9 %reshape.307 = f32[640,2,12,2,2,40]{5,4,3,2,1,0:T(2,128)} reshape(f32[8,307200]{1,0:T(8,128)} %reduce.2) | data formatting | bytes 19660800
  1849.2 36.9 %copy.77 = f32[40,2,12,2,2,8,80]{6,0,5,4,3,2,1:T(8,128)} copy(f32[40,2,12,2,2,8,80]{0,4,3,2,1,6,5:T(2,128)} %bitcast.86) | data formatting | bytes 19660800 | tf_op jit(solution)/shard_map/all_to_all | solution.py:72
  1903.3 90.7 %reduce.3 = f32[8,307200]{1,0:T(8,128)} reduce(f32[8,1,307200]{2,1,0:T(1,128)} %all-to-all-done.3, f32[]{:T(128)} %broadcast.351), dimensions={1}, to_apply=%all_to_all.64.reduce_sub_computation | reduce | bytes 19660804 | tf_op jit(solution)/shard_map/all_to_all | solution.py:72
  1993.9 83.9 %reshape.309 = f32[640,2,12,2,2,40]{5,4,3,2,1,0:T(2,128)} reshape(f32[8,307200]{1,0:T(8,128)} %reduce.3) | data formatting | bytes 19660800
  2077.9 36.9 %copy.79 = f32[40,2,12,2,2,8,80]{6,0,5,4,3,2,1:T(8,128)} copy(f32[40,2,12,2,2,8,80]{0,4,3,2,1,6,5:T(2,128)} %bitcast.87) | data formatting | bytes 19660800 | tf_op jit(solution)/shard_map/all_to_all | solution.py:72
  2149.1 90.8 %reduce = f32[8,307200]{1,0:T(8,128)} reduce(f32[8,1,307200]{2,1,0:T(1,128)} %all-to-all-done, f32[]{:T(128)} %broadcast.351), dimensions={1}, to_apply=%all_to_all.52.reduce_sub_computation | reduce | bytes 19660804 | tf_op jit(solution)/shard_map/all_to_all | solution.py:72
  2239.9 83.9 %reshape.303 = f32[640,2,12,2,2,40]{5,4,3,2,1,0:T(2,128)} reshape(f32[8,307200]{1,0:T(8,128)} %reduce) | data formatting | bytes 19660800
  2323.9 36.9 %copy.73 = f32[40,2,12,2,2,8,80]{6,0,5,4,3,2,1:T(8,128)} copy(f32[40,2,12,2,2,8,80]{0,4,3,2,1,6,5:T(2,128)} %bitcast.88) | data formatting | bytes 19660800 | tf_op jit(solution)/shard_map/all_to_all | solution.py:72
  2431.1 162.5 %multiply_reduce_fusion = (f32[2,48]{1,0:T(2,128)S(1)}, f32[2,48,80,1280]{3,2,1,0:T(8,128)}) fusion(f32[320,2,48,2,2,80]{0,5,4,3,2,1:T(8,128)} %constant_dynamic-update-slice_fusion, f32[320,2,2,1280,1,1]{3,0,2,1,5,4:T(8,128)S(1)} %bitcast.94), kind=kOutput, calls=%fused_computation.4 | convolution fusion | flops 151014604800 | bytes 85197184 | tf_op jit(solution)/shard_map/dot_general | solution.py:91
  (52 shorter events, 229.7 us)
Async XLA Ops:
  350.0 40.5 %copy-start.1 = (s32[8]{0:T(128)S(1)}, s32[8]{0:T(128)}, u32[]{:S(2)}) copy-start(s32[8]{0:T(128)} %param.7) | copy-start | bytes 100
  778.0 221.6 %all-to-all-start.1 = ((f32[8,1,307200]{2,1,0:T(1,128)}), f32[8,1,307200]{2,1,0:T(1,128)}, u32[]{:S(2)}, u32[]{:S(2)}) async-start(f32[8,1,307200]{2,1,0:T(1,128)} %reshape.304), calls=%async_computation.1 | async-start | bytes 19660800 | tf_op jit(solution)/shard_map/all_to_all | solution.py:72
  999.6 220.1 %all-to-all-start.2 = ((f32[8,1,307200]{2,1,0:T(1,128)}), f32[8,1,307200]{2,1,0:T(1,128)}, u32[]{:S(2)}, u32[]{:S(2)}) async-start(f32[8,1,307200]{2,1,0:T(1,128)} %reshape.306), calls=%async_computation.2 | async-start | bytes 19660800 | tf_op jit(solution)/shard_map/all_to_all | solution.py:72
  1219.7 220.3 %all-to-all-start.3 = ((f32[8,1,307200]{2,1,0:T(1,128)}), f32[8,1,307200]{2,1,0:T(1,128)}, u32[]{:S(2)}, u32[]{:S(2)}) async-start(f32[8,1,307200]{2,1,0:T(1,128)} %reshape.308), calls=%async_computation.3 | async-start | bytes 19660800 | tf_op jit(solution)/shard_map/all_to_all | solution.py:72
  1440.0 709.1 %all-to-all-start = ((f32[8,1,307200]{2,1,0:T(1,128)}), f32[8,1,307200]{2,1,0:T(1,128)}, u32[]{:S(2)}, u32[]{:S(2)}) async-start(f32[8,1,307200]{2,1,0:T(1,128)} %reshape.302), calls=%async_computation | async-start | bytes 19660800 | tf_op jit(solution)/shard_map/all_to_all | solution.py:72
  1672.9 728.6 %collective-permute-start = (f32[320,2,12,2,2,80]{0,5,4,3,2,1:T(8,128)}, f32[320,2,12,2,2,80]{0,5,4,3,2,1:T(8,128)}, u32[]{:S(2)}, u32[]{:S(2)}) collective-permute-start(f32[320,2,12,2,2,80]{0,5,4,3,2,1:T(8,128)} %copy.56), channel_id=1, source_target_pairs={{0,8},{8,16},{16,24},{24,0},{1,9},{9,17},{17,25},{25,1},{2,10},{10... | collective-permute-start | bytes 29491208 | tf_op jit(solution)/shard_map/ppermute | solution.py:19
  1901.8 509.7 %collective-permute-start.1 = (f32[320,2,12,2,2,80]{0,5,4,3,2,1:T(8,128)}, f32[320,2,12,2,2,80]{0,5,4,3,2,1:T(8,128)}, u32[]{:S(2)}, u32[]{:S(2)}) collective-permute-start(f32[320,2,12,2,2,80]{0,5,4,3,2,1:T(8,128)} %copy.60), channel_id=1, source_target_pairs={{0,16},{8,24},{16,0},{24,8},{1,17},{9,25},{17,1},{25,9},{2,18},{10... | collective-permute-start | bytes 29491208 | tf_op jit(solution)/shard_map/ppermute | solution.py:19
  2077.9 54.1 %copy-start = (s32[320]{0:T(512)S(1)}, s32[320]{0:T(512)}, u32[]{:S(2)}) copy-start(s32[320]{0:T(512)} %param.6) | copy-start | bytes 3844
  2130.5 290.8 %collective-permute-start.2 = (f32[320,2,12,2,2,80]{0,5,4,3,2,1:T(8,128)}, f32[320,2,12,2,2,80]{0,5,4,3,2,1:T(8,128)}, u32[]{:S(2)}, u32[]{:S(2)}) collective-permute-start(f32[320,2,12,2,2,80]{0,5,4,3,2,1:T(8,128)} %copy.64), channel_id=1, source_target_pairs={{0,24},{8,0},{16,8},{24,16},{1,25},{9,1},{17,9},{25,17},{2,26},{10... | collective-permute-start | bytes 29491208 | tf_op jit(solution)/shard_map/ppermute | solution.py:19
  2401.5 29.6 %slice-start = ((s8[6553600]{0:T(1024)(128)(4,1)}), s8[4194304]{0:T(1024)(128)(4,1)S(1)}, s32[]{:S(2)}) async-start(s8[6553600]{0:T(1024)(128)(4,1)} %bitcast.93), calls=%async_computation.4 | async-start | bytes 8388608
  2411.4 19.7 slice-start.1
where the time goes:
time: 2670 us; the launch traced here: 2620 us
  local copies, waits for them, and re-layouts  1470 us (55%)
  matrix products  544 us (20%)
  other arithmetic  489 us (18%)
  waiting for transfers between devices  62.1 us (2%)
  starting transfers between devices  27.5 us (1%)
    unnamed x17, local copies, waits for them, and re-layouts  628 us
    rev x2, local copies, waits for them, and re-layouts, legendre_table(): south = (belong * signs)[..., None] * jnp.flip(legendre, -1)[:, :, None, :]  388 us
    dot_general x4, matrix products, legendre_sums(): lax.dot_general(coeffs, table, (((4,), (1,)), ((2,), (0,))), precision=HI...  381 us
    all_to_all x4, other arithmetic, local(): lax.all_to_all(fourier, 'wide', split_axis=5, concat_axis=0, tiled=True)  363 us
    all_to_all x9, local copies, waits for them, and re-layouts, local(): lax.all_to_all(fourier, 'wide', split_axis=5, concat_axis=0, tiled=True)  211 us
    dot_general x1, matrix products, local(): lax.dot_general(arrived, synthesis, (((0, 3, 4), (0, 1, 2)), ((), ())), p...  162 us
    dot_general x4, local copies, waits for them, and re-layouts, legendre_sums(): lax.dot_general(coeffs, table, (((4,), (1,)), ((2,), (0,))), precision=HI...  144 us
    mul x2, other arithmetic, legendre_table(): south = (belong * signs)[..., None] * jnp.flip(legendre, -1)[:, :, None, :]  79.6 us
  transfers between devices with their start and end apart: 7, of which 3 were waited for; matrix products, arithmetic and copies ran while one was open for 59% of the time, Pallas kernels for 0%

commit v1 on v0

v1 whole, which is shorter than its diff:
```python
import math

import jax
import jax.numpy as jnp
from jax import lax
from jax.sharding import PartitionSpec as P

WAVES = 640
LAT = 640
LON = 1280


HIGH = lax.Precision.HIGH
MOST_CHUNKS = 4


def coefficient_weights(slot_pairs, coeff_count):
    degree = jnp.arange(coeff_count, dtype=jnp.int32)[None, :]
    boundary = (WAVES - slot_pairs)[:, None]
    first_part = degree < boundary
    within = jnp.where(first_part, degree, degree - boundary)
    sign = jnp.where(within % 2 == 0, 1.0, -1.0).astype(jnp.float32)
    pair_even = (slot_pairs % 2 == 0)[:, None]
    even_wave = (first_part == pair_even).astype(jnp.float32)
    belong = jnp.stack([even_wave, 1.0 - even_wave], 1)
    return belong, belong * sign[:, None, :]


def legendre_sums(coeffs, weights, legendre):
    by_slot = jnp.transpose(coeffs, (2, 3, 0, 1, 4))
    masked = weights[:, :, None, None, None, :] * by_slot[:, None]
    slots, _, _, _, _, depth = masked.shape
    masked = masked.reshape(slots, -1, depth)
    return lax.dot_general(
        legendre,
        masked,
        (((1,), (2,)), ((0,), (0,))),
        precision=HIGH,
        preferred_element_type=jnp.float32,
    )


def synthesis_table(pairs):
    other = WAVES - 1 - pairs
    even = pairs % 2 == 0
    numbers = jnp.stack([jnp.where(even, pairs, other), jnp.where(even, other, pairs)], 0)
    columns = jnp.arange(LON // 2, dtype=jnp.int32)
    phases = numbers[:, :, None] * columns % LON
    angles = phases.astype(jnp.float32) * (2.0 * math.pi / LON)
    factor = jnp.where(numbers == 0, 1.0, 2.0).astype(jnp.float32)[:, :, None]
    return jnp.stack([factor * jnp.cos(angles), -factor * jnp.sin(angles)], 2)


def local(spectral, legendre, pair_table, field_map):
    slot_count = legendre.shape[0]
    coeff_count = legendre.shape[1]
    wide = lax.axis_size("wide")
    chunks = max(n for n in range(1, MOST_CHUNKS + 1) if slot_count % n == 0)
    size = slot_count // chunks
    own_pairs = lax.dynamic_slice_in_dim(
        pair_table, lax.axis_index("wide") * slot_count, slot_count
    )
    north_weights, south_weights = coefficient_weights(own_pairs, coeff_count)
    fields = None
    levels = None
    arrived = []
    for chunk in range(chunks):
        start, stop = chunk * size, (chunk + 1) * size
        part = jnp.take(spectral[:, :, start:stop], field_map, axis=0)
        part = lax.all_to_all(part, "grp", split_axis=0, concat_axis=1, tiled=True)
        fields, levels = part.shape[0], part.shape[1]
        table = legendre[start:stop]
        north = legendre_sums(part, north_weights[start:stop], table)
        south = legendre_sums(part, south_weights[start:stop], jnp.flip(table, -1))
        fourier = jnp.concatenate([north, south], 1)
        arrived.append(
            lax.all_to_all(fourier, "wide", split_axis=1, concat_axis=0, tiled=True)
        )
    collected = jnp.concatenate(arrived, 0)
    slots, band = collected.shape[0], collected.shape[1]
    collected = collected.reshape(slots, band, 2, 2, fields, levels)
    ordered_pairs = pair_table.reshape(wide, chunks, size).transpose(1, 0, 2).reshape(-1)
    synthesis = synthesis_table(ordered_pairs)
    halves = [
        lax.dot_general(
            collected[:, :, parity],
            synthesis[parity],
            (((0, 2), (0, 1)), ((), ())),
            precision=HIGH,
            preferred_element_type=jnp.float32,
        )
        for parity in range(2)
    ]
    even, odd = [jnp.transpose(half, (1, 2, 0, 3)) for half in halves]
    gridded = jnp.concatenate([even + odd, even - odd], -1)
    local_sum = 2.0 * jnp.sum(even * even + odd * odd, axis=(2, 3))
    summed = lax.psum(local_sum, "wide")
    checksums = lax.all_gather(summed, "grp", axis=0, tiled=True) / (LAT * LON)
    return (gridded, checksums)


def solution(mesh):
    placed = (P(None, "grp", "wide", None, None), P("wide", None, None), P(), P())
    return jax.shard_map(
        local,
        mesh=mesh,
        in_specs=placed,
        out_specs=(P("grp", None, "wide", None), P()),
        check_vma=False,
    )
```

time: 2670 us -> 2130 us (0.80)
  local copies, waits for them, and re-layouts: 1470 us -> 721 us
  waiting for transfers between devices: 62.1 us -> 791 us
  matrix products: 544 us -> 217 us
  other arithmetic: 489 us -> 162 us
  blocking collectives: 23.3 us -> 163 us
    all_to_all x4 -> x6, waiting for transfers between devices: 62.1 us -> 791 us  [the longest x4 755 us: local(): lax.all_to_all(fourier, 'wide', split_axis=1, concat_axis=0, tiled=True)]
    unnamed x17 -> x9, local copies, waits for them, and re-layouts: 628 us -> 36.9 us
    all_to_all x4 -> x0, other arithmetic: 363 us -> none  [local(): lax.all_to_all(fourier, 'wide', split_axis=5, concat_axis=0, tiled=True)]
    dot_general x5 -> x10, matrix products: 544 us -> 217 us  [the longest x8 148 us: legendre_sums(): lax.dot_general(legendre, masked, (((1,), (2,)), ((0,), (0,))), precision...]
    dot_general x4 -> x0, local copies, waits for them, and re-layouts: 144 us -> none  [legendre_sums(): lax.dot_general(coeffs, table, (((4,), (1,)), ((2,), (0,))), precision=HI...]
    concatenate x0 -> x8, local copies, waits for them, and re-layouts: none -> 143 us  [the longest x4 81.3 us: local(): collected = jnp.concatenate(arrived, 0)]
    all_to_all x0 -> x2, blocking collectives: none -> 140 us  [local(): part = lax.all_to_all(part, 'grp', split_axis=0, concat_axis=1, tiled=True)]
    all_to_all x9 -> x8, local copies, waits for them, and re-layouts: 211 us -> 85.6 us  [the longest x4 66.8 us: local(): lax.all_to_all(fourier, 'wide', split_axis=1, concat_axis=0, tiled=True)]
  transfers between devices with their start and end apart: 7 -> 6, of which waited for: 3 -> 5; matrix products, arithmetic and copies ran while one was open for 59% -> 38% of each run, Pallas kernels for 0% -> 0%
where the time goes in v1:
time: 2130 us; the launch traced here: 2090 us
  waiting for transfers between devices  791 us (37%)
  local copies, waits for them, and re-layouts  721 us (34%)
  matrix products  217 us (10%)
  blocking collectives  163 us (8%)
  other arithmetic  162 us (8%)
  starting transfers between devices  34.1 us (2%)
    all_to_all x4, waiting for transfers between devices, local(): lax.all_to_all(fourier, 'wide', split_axis=1, concat_axis=0, tiled=True)  755 us
    rev x4, local copies, waits for them, and re-layouts, local(): south = legendre_sums(part, south_weights[start:stop], jnp.flip(table, -1))  352 us
    dot_general x8, matrix products, legendre_sums(): lax.dot_general(legendre, masked, (((1,), (2,)), ((0,), (0,))), precision...  148 us
    all_to_all x2, blocking collectives, local(): part = lax.all_to_all(part, 'grp', split_axis=0, concat_axis=1, tiled=True)  140 us
    concatenate x4, local copies, waits for them, and re-layouts, local(): collected = jnp.concatenate(arrived, 0)  81.3 us
    dot_general x2, matrix products, local(): lax.dot_general(collected[:, :, parity], synthesis[parity], (((0, 2), (0,...  69.3 us
    all_to_all x4, local copies, waits for them, and re-layouts, local(): lax.all_to_all(fourier, 'wide', split_axis=1, concat_axis=0, tiled=True)  66.8 us
    concatenate x4, local copies, waits for them, and re-layouts, local(): fourier = jnp.concatenate([north, south], 1)  62 us
  transfers between devices with their start and end apart: 6, of which 5 were waited for; matrix products, arithmetic and copies ran while one was open for 38% of the time, Pallas kernels for 0%

profile of v1, /device:TPU:0, one launch (start us, length us, event | category | flops | bytes accessed | tf_op | source)
XLA Modules:
  0.0 2089.1 jit_solution(1974635825256463929)
XLA Ops:
  2.0 19.2 fusion.38
  71.8 16.8 broadcast_select_fusion.3
  88.6 71.2 %all_to_all.132 = f32[8,12,10,2,641]{4,3,2,1,0:T(2,128)} all-to-all(f32[8,12,10,2,641]{4,3,2,1,0:T(2,128)S(1)} %get-tuple-element.48), channel_id=1, replica_groups=mesh['grp'=4,'wide'=8] {'grp'}, dimensions={0} | all-to-all | bytes 9845760 | tf_op jit(solution)/shard_map/all_to_all | solution.py:70
  159.8 68.6 %all_to_all.133 = f32[8,12,10,2,641]{4,3,2,1,0:T(2,128)} all-to-all(f32[8,12,10,2,641]{4,3,2,1,0:T(2,128)S(1)} %get-tuple-element.49), channel_id=1, replica_groups=mesh['grp'=4,'wide'=8] {'grp'}, dimensions={0} | all-to-all | bytes 9845760 | tf_op jit(solution)/shard_map/all_to_all | solution.py:70
  234.1 26.7 %fusion.37 = (f32[10,641,320]{1,2,0:T(8,128)}, f32[10,641,320]{1,2,0:T(8,128)}, f32[10,641,320]{1,2,0:T(8,128)}, f32[10,641,320]{1,2,0:T(8,128)}) fusion(f32[40,641,320]{1,2,0:T(8,128)} %param.7), kind=kLoop, calls=%fused_computation.109 | loop fusion | bytes 65638400 | tf_op jit(solution)/shard_map/slice | solution.py:72
  260.8 35.8 %all-to-all-done.4 = f32[8,12,10,2,641]{4,3,2,1,0:T(2,128)} async-done(((f32[8,12,10,2,641]{4,3,2,1,0:T(2,128)}), f32[8,12,10,2,641]{4,3,2,1,0:T(2,128)}, u32[]{:S(2)}, u32[]{:S(2)}) %all-to-all-start.4) | async-done | bytes 4922912 | tf_op jit(solution)/shard_map/all_to_all | solution.py:70
  303.5 88.1 %rev.13 = f32[10,641,320]{1,2,0:T(8,128)} reverse(f32[10,641,320]{1,2,0:T(8,128)} %get-tuple-element.20), dimensions={2} | reverse | bytes 16409600 | tf_op jit(solution)/shard_map/jit(_flip)/rev | solution.py:74
  406.6 18.2 convolution_bitcast_fusion.7
  424.8 18.9 convolution_bitcast_fusion.6
  473.6 88.1 %rev.14 = f32[10,641,320]{1,2,0:T(8,128)} reverse(f32[10,641,320]{1,2,0:T(8,128)} %get-tuple-element.21), dimensions={2} | reverse | bytes 16409600 | tf_op jit(solution)/shard_map/jit(_flip)/rev | solution.py:74
  576.7 18.2 convolution_bitcast_fusion.5
  594.8 18.6 convolution_bitcast_fusion.4
  637.4 177.2 %all-to-all-done.1 = f32[10,640,384]{2,0,1:T(8,128)} async-done(((f32[10,640,384]{2,0,1:T(8,128)}), f32[10,640,384]{2,0,1:T(8,128)}, u32[]{:S(2)}, u32[]{:S(2)}) %all-to-all-start.1) | async-done | bytes 9830432 | tf_op jit(solution)/shard_map/all_to_all | solution.py:77
  820.8 88.1 %rev.15 = f32[10,641,320]{1,2,0:T(8,128)} reverse(f32[10,641,320]{1,2,0:T(8,128)} %get-tuple-element.23), dimensions={2} | reverse | bytes 16409600 | tf_op jit(solution)/shard_map/jit(_flip)/rev | solution.py:74
  923.7 18.2 convolution_bitcast_fusion.3
  941.9 18.6 convolution_bitcast_fusion.2
  984.0 177.8 %all-to-all-done.3 = f32[10,640,384]{2,0,1:T(8,128)} async-done(((f32[10,640,384]{2,0,1:T(8,128)}), f32[10,640,384]{2,0,1:T(8,128)}, u32[]{:S(2)}, u32[]{:S(2)}) %all-to-all-start.3) | async-done | bytes 9830432 | tf_op jit(solution)/shard_map/all_to_all | solution.py:77
  1167.9 88.1 %rev.16 = f32[10,641,320]{1,2,0:T(8,128)} reverse(f32[10,641,320]{1,2,0:T(8,128)} %get-tuple-element.22), dimensions={2} | reverse | bytes 16409600 | tf_op jit(solution)/shard_map/jit(_flip)/rev | solution.py:74
  1271.0 18.3 convolution_bitcast_fusion.1
  1289.2 18.6 convolution_bitcast_fusion
  1331.9 177.0 %all-to-all-done.5 = f32[10,640,384]{2,0,1:T(8,128)} async-done(((f32[10,640,384]{2,0,1:T(8,128)}), f32[10,640,384]{2,0,1:T(8,128)}, u32[]{:S(2)}, u32[]{:S(2)}) %all-to-all-start.5) | async-done | bytes 9830432 | tf_op jit(solution)/shard_map/all_to_all | solution.py:77
  1538.5 20.3 copy.154
  1575.5 20.3 copy.155
  1612.4 20.3 copy.156
  1632.7 223.1 %all-to-all-done.7 = f32[10,640,384]{2,0,1:T(8,128)} async-done(((f32[10,640,384]{2,0,1:T(8,128)}), f32[10,640,384]{2,0,1:T(8,128)}, u32[]{:S(2)}, u32[]{:S(2)}) %all-to-all-start.7) | async-done | bytes 9830432 | tf_op jit(solution)/shard_map/all_to_all | solution.py:77
  1855.8 16.8 copy.153
  1872.6 20.3 copy.157
  1893.0 38.4 %pad_maximum_fusion = f32[320,80,2,2,2,48]{0,5,3,4,1,2:T(8,128)} fusion(f32[80,80,2,2,2,48]{0,5,3,4,1,2:T(8,128)} %copy.157, f32[80,80,2,2,2,48]{0,5,3,4,1,2:T(8,128)} %copy.156, f32[80,80,2,2,2,48]{0,5,3,4,1,2:T(8,128)} %copy.155, f32[80,80,2,2,2,48]{0,5,3,4,1,2:T(8,128)} %copy.154), kind=kLoop, calls=%fused_computation.4 | loop fusion | flops 29491200 | bytes 78643200 | tf_op jit(solution)/shard_map/concatenate | solution.py:79
  1931.4 31.8 %fusion = f32[80,2,48,640,1]{3,2,4,1,0:T(8,128)} fusion(f32[320,80,2,2,2,48]{0,5,3,4,1,2:T(8,128)} %pad_maximum_fusion, f32[2,320,1,640]{3,1,2,0:T(8,128)S(1)} %get-tuple-element.45, f32[2,320,1,640]{3,1,2,0:T(8,128)S(1)} %get-tuple-element.44), kind=kOutput, calls=%fused_computation.7 | convolution fusion | flops 18874777600 | bytes 46530560 | tf_op jit(solution)/shard_map/dot_general | solution.py:85
  1963.3 37.4 %fusion.5 = (f32[2,48]{1,0:T(2,128)S(1)}, f32[2,48,80,640]{3,1,0,2:T(8,128)}, f32[2,48,80,640]{3,1,0,2:T(8,128)}) fusion(f32[80,2,48,640,1]{3,2,4,1,0:T(8,128)} %fusion, f32[2,320,1,640]{3,1,2,0:T(8,128)S(1)} %get-tuple-element.44, f32[2,320,1,640]{3,1,2,0:T(8,128)S(1)} %get-tuple-element.45, f32[320,80,2,2,2,48]{0,5,3,4,1,2:T(8,128)} %pad_maximum_fusion), kind=kOutput, calls=%fused_computation.16 | convolution fusion | flops 18904268800 | bytes 85852544 | tf_op jit(solution)/shard_map/dot_general | solution.py:85
  2000.7 27.5 %pad_maximum_fusion.1 = f32[2,48,80,1280]{3,1,0,2:T(8,128)} fusion(f32[2,48,80,640]{3,1,0,2:T(8,128)} %get-tuple-element.18, f32[2,48,80,640]{3,1,0,2:T(8,128)} %get-tuple-element.19), kind=kLoop, calls=%fused_computation.5 | loop fusion | flops 9830400 | bytes 78643200 | tf_op jit(solution)/shard_map/concatenate | solution.py:95
  2028.2 36.8 %copy.159 = f32[2,48,80,1280]{3,2,1,0:T(8,128)} copy(f32[2,48,80,1280]{3,1,0,2:T(8,128)} %pad_maximum_fusion.1) | data formatting | bytes 78643200
  (73 shorter events, 324.3 us)
Async XLA Ops:
  159.8 73.8 %copy-start.2 = (s32[320]{0:T(512)S(1)}, s32[320]{0:T(512)}, u32[]{:S(2)}) copy-start(s32[320]{0:T(512)} %param.8) | copy-start | bytes 3844
  228.4 68.2 %all-to-all-start.4 = ((f32[8,12,10,2,641]{4,3,2,1,0:T(2,128)}), f32[8,12,10,2,641]{4,3,2,1,0:T(2,128)}, u32[]{:S(2)}, u32[]{:S(2)}) async-start(f32[8,12,10,2,641]{4,3,2,1,0:T(2,128)} %get-tuple-element.50), calls=%async_computation.4 | async-start | bytes 11796480 | tf_op jit(solution)/shard_map/all_to_all | solution.py:70
  296.6 171.0 %all-to-all-start.6 = ((f32[8,12,10,2,641]{4,3,2,1,0:T(2,128)}), f32[8,12,10,2,641]{4,3,2,1,0:T(2,128)}, u32[]{:S(2)}, u32[]{:S(2)}) async-start(f32[8,12,10,2,641]{4,3,2,1,0:T(2,128)} %get-tuple-element.51), calls=%async_computation.6 | async-start | bytes 11796480 | tf_op jit(solution)/shard_map/all_to_all | solution.py:70
  467.6 347.0 %all-to-all-start.1 = ((f32[10,640,384]{2,0,1:T(8,128)}), f32[10,640,384]{2,0,1:T(8,128)}, u32[]{:S(2)}, u32[]{:S(2)}) async-start(f32[10,640,384]{2,0,1:T(8,128)} %copy.124), calls=%async_computation.1 | async-start | bytes 31457280 | tf_op jit(solution)/shard_map/all_to_all | solution.py:77
  814.6 347.2 %all-to-all-start.3 = ((f32[10,640,384]{2,0,1:T(8,128)}), f32[10,640,384]{2,0,1:T(8,128)}, u32[]{:S(2)}, u32[]{:S(2)}) async-start(f32[10,640,384]{2,0,1:T(8,128)} %copy.133), calls=%async_computation.3 | async-start | bytes 31457280 | tf_op jit(solution)/shard_map/all_to_all | solution.py:77
  984.0 183.7 %copy-start = (f32[10,2,641]{2,0,1:T(8,128)S(1)}, f32[10,2,641]{2,0,1:T(8,128)}, u32[]{:S(2)}) copy-start(f32[10,2,641]{2,0,1:T(8,128)} %get-tuple-element.41) | copy-start | bytes 153844
  984.0 183.8 %copy-start.1 = (f32[10,2,641]{2,0,1:T(8,128)S(1)}, f32[10,2,641]{2,0,1:T(8,128)}, u32[]{:S(2)}) copy-start(f32[10,2,641]{2,0,1:T(8,128)} %get-tuple-element.39) | copy-start | bytes 153844
  1161.9 347.0 %all-to-all-start.5 = ((f32[10,640,384]{2,0,1:T(8,128)}), f32[10,640,384]{2,0,1:T(8,128)}, u32[]{:S(2)}, u32[]{:S(2)}) async-start(f32[10,640,384]{2,0,1:T(8,128)} %copy.142), calls=%async_computation.5 | async-start | bytes 31457280 | tf_op jit(solution)/shard_map/all_to_all | solution.py:77
  1331.9 182.8 %copy-start.3 = (s32[320]{0:T(512)S(1)}, s32[320]{0:T(512)}, u32[]{:S(2)}) copy-start(s32[320]{0:T(512)} %param.8) | copy-start | bytes 3844
  1508.9 347.0 %all-to-all-start.7 = ((f32[10,640,384]{2,0,1:T(8,128)}), f32[10,640,384]{2,0,1:T(8,128)}, u32[]{:S(2)}, u32[]{:S(2)}) async-start(f32[10,640,384]{2,0,1:T(8,128)} %copy.151), calls=%async_computation.7 | async-start | bytes 31457280 | tf_op jit(solution)/shard_map/all_to_all | solution.py:77
